TPU v7x, 32 devices: a whole 2x2x4 slice. The times are simulated.
32 devices in a mesh: grp: 2 (over x), row: 16 (over z, y, core).
Axes of the slice: x: 2, y: 2, z: 4, core: 2. Of those that a mesh axis runs over, the one named last changes fastest.
Arguments:
- members_in: bfloat16 [256, 4096], P(('grp', 'row')), parts along dimension 0, may hold values from -6 to 6
- gate_up: bfloat16 [4096, 2, 14336], P(None, None, 'row'), may hold values from -0.09375 to 0.09375
- down_weight: bfloat16 [14336, 4096], P('row'), may hold values from -0.046875 to 0.046875
- factor_in: bfloat16 [256, 4, 4096], P('grp', None, 'row'), parts along dimension 0, may hold values from -0.09375 to 0.09375
- factor_out: bfloat16 [256, 4, 2, 14336], P('grp', None, None, 'row'), parts along dimension 0, may hold values from -6 to 6
- target: float32 [256, 4096], P(('grp', 'row')), parts along dimension 0, may hold values from -6 to 6
Outputs:
- outputs: bfloat16 [256, 4096], P(('grp', 'row')), parts along dimension 0
- fitness: float32 [256], P(('grp', 'row')), parts along dimension 0
- update: float32 [8192, 2, 14336], P('grp', None, 'row'), parts along dimension 0
There are 2 independent parts, one for each index of `grp`. A program takes and returns all parts, laid end to end along the dimension named above; an argument that names none is the same for every part. Nothing has to cross between parts.
All inputs are finite; a program needn't handle non-finite values.
Results may differ from a plain program's by a relative error of at most 0.0049.
Values may be sent and summed in bfloat16 or wider, within the bound.
A program may use at most 128 MiB of HBM per device.

v0:
```python
import math

import jax
import jax.numpy as jnp
from jax import lax
from jax.sharding import PartitionSpec as P

noise_scale = 0.5


def body(members_in, gate_up, down_weight, factor_in, factor_out, target):
    own_rows = members_in.shape[0]
    width = gate_up.shape[0]
    local_units = gate_up.shape[2]
    members = factor_in.shape[0]
    rank = factor_in.shape[1]
    whole_x = lax.all_gather(members_in, "row", axis=0, tiled=True)
    full_factor = lax.all_gather(factor_in, "row", axis=2, tiled=True)
    projected = jnp.einsum("md,mrd->mr", whole_x, full_factor, preferred_element_type=jnp.float32)
    stacked = jnp.dot(
        whole_x, gate_up.reshape(width, 2 * local_units), preferred_element_type=jnp.float32
    )
    stacked = stacked.reshape(members, 2, local_units)
    noise = jnp.sum(projected[:, :, None, None] * factor_out, axis=1)
    stacked = stacked + noise * (noise_scale / math.sqrt(rank))
    hidden = (jax.nn.silu(stacked[:, 0]) * stacked[:, 1]).astype(jnp.bfloat16)
    sums = lax.psum_scatter(
        jnp.dot(hidden, down_weight, preferred_element_type=jnp.float32),
        "row",
        scatter_dimension=0,
        tiled=True,
    )
    own_losses = jnp.mean((sums - target) ** 2, axis=1)
    losses = lax.all_gather(own_losses, "row", axis=0, tiled=True)
    average = jnp.mean(losses)
    spread = jnp.mean((losses - average) ** 2)
    all_fitness = (average - losses) / jnp.sqrt(spread + 1e-06)
    own_fitness = lax.dynamic_slice_in_dim(
        all_fitness, lax.axis_index("row") * own_rows, own_rows, 0
    )
    scaled = (all_fitness[:, None, None, None] * factor_out).astype(jnp.bfloat16)
    step_scale = math.sqrt(width / (members * rank))
    contract = (((0, 1), (0, 1)), ((), ()))
    update = lax.dot_general(full_factor, scaled, contract, preferred_element_type=jnp.float32)
    update = update * step_scale
    return (sums.astype(jnp.bfloat16), own_fitness, update)


def solution(mesh):
    return jax.shard_map(
        body,
        mesh=mesh,
        in_specs=(
            P(("grp", "row"), None),
            P(None, None, "row"),
            P("row", None),
            P("grp", None, "row"),
            P("grp", None, None, "row"),
            P(("grp", "row"), None),
        ),
        out_specs=(P(("grp", "row"), None), P(("grp", "row")), P("grp", None, "row")),
        check_vma=False,
    )
```

profile of v0, /device:TPU:0, one launch (start us, length us, event | category | flops | bytes accessed | tf_op | source)
XLA Modules:
  0.0 292.8 jit_solution(10210065390690066654)
XLA Ops:
  7.2 0.0 all-gather.3.cloned.1.call-start
  7.2 0.7 all-gather.3.cloned.1.call-update
  7.9 0.0 all-gather.5.cloned.1.call-start
  7.9 1.7 copy.14
  9.6 0.0 all-gather.5.cloned.1.call-update
  9.7 0.0 reduce-scatter.2.cloned.1.call-start
  9.7 15.9 %copy.22 = bf16[512,8,2,896]{3,1,2,0:T(8,128)(2,1)} copy(bf16[512,8,2,896]{3,2,1,0:T(2,128)(2,1)} %bitcast.37) | data formatting | bytes 29360128
  25.6 19.6 %copy.13 = bf16[1792,4096]{1,0:T(8,128)(2,1)} copy(bf16[1792,4096]{0,1:T(8,128)(2,1)} %bitcast.36) | data formatting | bytes 29360128 | tf_op jit(solution)/shard_map/dot_general | solution.py:20
  45.2 5.5 %all-gather.3.cloned.1.call-done = bf16[128,4096]{1,0:T(8,128)(2,1)} async-done(((bf16[8,4096]{1,0:T(8,128)(2,1)}), bf16[128,4096]{1,0:T(8,128)(2,1)}) %all-gather.3.cloned.1.call-update) | async-done | bytes 1048592 | tf_op jit(solution)/shard_map/all_gather | solution.py:17
  50.8 53.6 %all-gather.5.cloned.1.call-done = bf16[128,4,4096]{2,0,1:T(8,128)(2,1)} async-done(((bf16[128,4,256]{2,0,1:T(8,128)(2,1)}), bf16[128,4,4096]{2,0,1:T(8,128)(2,1)}) %all-gather.5.cloned.1.call-update) | async-done | bytes 4194320 | tf_op jit(solution)/shard_map/all_gather | solution.py:18
  104.4 0.0 copy-start
  104.4 0.0 copy-start.1
  104.4 8.4 %fusion.2 = f32[128,1,4]{2,1,0:T(1,128)S(1)} fusion(bf16[128,4,4096]{2,0,1:T(8,128)(2,1)} %all-gather.5.cloned.1.call-done, bf16[128,4096,1]{1,0,2:T(8,128)(2,1)} %bitcast.38), kind=kOutput, calls=%fused_computation.5 | convolution fusion | flops 4194304 | bytes 5244928 | tf_op jit(solution)/shard_map/md,mrd->mr/dot_general | solution.py:19
  112.8 0.0 copy-done
  112.8 2.4 fusion.4
  115.2 0.0 copy-done.1
  115.2 10.2 %convolution_add_fusion = f32[128,2,896]{2,0,1:T(8,128)S(1)} fusion(bf16[2,896,4096]{2,1,0:T(8,128)(2,1)} %bitcast.35, f32[128,2,896]{2,1,0:T(2,128)S(1)} %fusion.4, bf16[128,4096]{1,0:T(8,128)(2,1)S(1)} %copy-done.1), kind=kOutput, calls=%fused_computation.11 | convolution fusion | flops 1879506944 | bytes 17563648 | tf_op jit(solution)/shard_map/dot_general | solution.py:20
  125.3 0.0 copy-start.3
  125.4 0.0 copy-start.2
  125.4 5.7 %fusion.10 = f32[128,4096]{1,0:T(8,128)} fusion(bf16[896,4096]{1,0:T(8,128)(2,1)} %param.8, f32[128,2,896]{2,0,1:T(8,128)S(1)} %convolution_add_fusion), kind=kOutput, calls=%fused_computation.17 | convolution fusion | flops 940212224 | bytes 10354688 | tf_op jit(solution)/shard_map/dot_general | solution.py:28
  131.1 0.0 reduce-scatter.2.cloned.1.call-update
  131.1 0.0 copy-done.3
  131.1 0.6 dynamic-slice
  132.4 58.9 %reduce-scatter.2.cloned.1.call-done = f32[8,4096]{1,0:T(8,128)} async-done(((f32[128,4096]{1,0:T(8,128)}), f32[8,4096]{1,0:T(8,128)}) %reduce-scatter.2.cloned.1.call-update) | async-done | bytes 131088 | tf_op jit(solution)/shard_map/reduce_scatter | solution.py:27
  191.2 0.0 copy-done.2
  191.2 1.7 multiply_reduce_fusion
  193.0 0.1 multiply_dynamic-update-slice_fusion
  193.1 29.7 %all-reduce = f32[128]{0:T(128)S(1)} all-reduce(f32[128]{0:T(128)S(1)} %multiply_dynamic-update-slice_fusion), channel_id=1, replica_groups=mesh['grp'=2,'row'=16] {'row'}, use_global_device_ids=true, to_apply=%add | all-reduce | flops 128 | bytes 1024
  222.7 0.6 reduce_sum.38
  224.0 0.6 multiply_reduce_fusion.1
  225.3 1.8 fusion.5
  227.1 0.6 dynamic_slice.3
  227.7 15.8 %fusion = f32[4096,2,896]{0,2,1:T(8,128)} fusion(bf16[128,4,4096]{2,0,1:T(8,128)(2,1)} %all-gather.5.cloned.1.call-done, bf16[128,4,2,896]{3,2,1,0:T(2,128)(2,1)S(1)} %fusion.5), kind=kOutput, calls=%fused_computation.1 | convolution fusion | flops 7523532800 | bytes 35389440 | tf_op jit(solution)/shard_map/dot_general | solution.py:44
  243.5 42.8 %copy.17 = f32[4096,2,896]{2,1,0:T(2,128)} copy(f32[4096,2,896]{0,2,1:T(8,128)} %fusion) | data formatting | bytes 58720256
  (2 shorter events, 0.0 us)
Async XLA Ops:
  7.2 43.6 %all-gather.3.cloned.1.call-start = ((), (), s32[]{:S(2)}) async-start(), calls=%async_computation.1 | async-start | bytes 1114112 | tf_op jit(solution)/shard_map/all_gather | solution.py:17
  7.9 96.5 %all-gather.5.cloned.1.call-start = ((), (), s32[]{:S(2)}) async-start(), calls=%async_computation.2 | async-start | bytes 4456448 | tf_op jit(solution)/shard_map/all_gather | solution.py:18
  9.7 181.6 %reduce-scatter.2.cloned.1.call-start = ((), (), s32[]{:S(2)}) async-start(), calls=%async_computation.3 | async-start | bytes 2228224 | tf_op jit(solution)/shard_map/reduce_scatter | solution.py:27
  104.4 8.4 %copy-start = (bf16[128,4,2,896]{3,2,1,0:T(2,128)(2,1)S(1)}, bf16[128,4,2,896]{3,2,1,0:T(2,128)(2,1)}, u32[]{:S(2)}) copy-start(bf16[128,4,2,896]{3,2,1,0:T(2,128)(2,1)} %param.10) | copy-start | bytes 5505028
  104.4 10.8 %copy-start.1 = (bf16[128,4096]{1,0:T(8,128)(2,1)S(1)}, bf16[128,4096]{1,0:T(8,128)(2,1)}, u32[]{:S(2)}) copy-start(bf16[128,4096]{1,0:T(8,128)(2,1)} %all-gather.3.cloned.1.call-done) | copy-start | bytes 3145732
  125.3 5.8 %copy-start.3 = (u32[32]{0:T(128)S(1)}, u32[32]{0:T(128)}, u32[]{:S(2)}) copy-start(u32[32]{0:T(128)} %constant.32) | copy-start | bytes 388
  125.4 65.9 %copy-start.2 = (f32[8,4096]{1,0:T(8,128)S(1)}, f32[8,4096]{1,0:T(8,128)}, u32[]{:S(2)}) copy-start(f32[8,4096]{1,0:T(8,128)} %param.11) | copy-start | bytes 393220
Sparse Core Ops, SparseCore 0:
  10.1 40.5 all-gather.2
  52.9 51.4 all-gather.4
  131.3 59.9 reduce-scatter.1
where the time goes:
time: 295 us; the launch traced here: 293 us
  waiting for transfers between devices  119 us (40%)
  local copies, waits for them, and re-layouts  81.2 us (28%)
  matrix products  40.1 us (14%)
  blocking collectives  29.7 us (10%)
  between operations  15.8 us (5%)
  other arithmetic  7.23 us (2%)
    unnamed x13, local copies, waits for them, and re-layouts  60.9 us
    reduce_scatter x1, waiting for transfers between devices, body(): lax.psum_scatter(jnp.dot(hidden, down_weight, preferred_element_type=jnp....  58.9 us
    all_gather x1, waiting for transfers between devices, body(): full_factor = lax.all_gather(factor_in, 'row', axis=2, tiled=True)  53.6 us
    unnamed x1, blocking collectives  29.7 us
    dot_general x1, local copies, waits for them, and re-layouts, body(): jnp.dot(whole_x, gate_up.reshape(width, 2 * local_units), preferred_eleme...  19.6 us
    dot_general x1, matrix products, body(): lax.dot_general(full_factor, scaled, contract, preferred_element_type=jnp...  15.8 us
    dot_general x1, matrix products, body(): jnp.dot(whole_x, gate_up.reshape(width, 2 * local_units), preferred_eleme...  10.2 us
    dot_general x1, matrix products, body(): jnp.einsum('md,mrd->mr', whole_x, full_factor, preferred_element_type=jnp...  8.38 us
  transfers between devices with their start and end apart: 3, of which 3 were waited for; matrix products, arithmetic and copies ran while one was open for 13% of the time, Pallas kernels for 0%

commit v1 on v0

--- a/solution.py
+++ b/solution.py
@@ -1,14 +1,505 @@
+import functools
 import math
 
 import jax
 import jax.numpy as jnp
 from jax import lax
+from jax.experimental import pallas as pl
+from jax.experimental.pallas import tpu as pltpu
 from jax.sharding import PartitionSpec as P
 
 noise_scale = 0.5
-
-
-def body(members_in, gate_up, down_weight, factor_in, factor_out, target):
+MESH = pl.DeviceIdType.MESH
+LANES = 128
+VMEM_LIMIT = 62 * 1024 * 1024
+
+
+class Gather:
+    def __init__(self, depth, place, own, slots, send_sems, recv_sems, local_sem):
+        self.depth, self.place = depth, place
+        self.own, self.slots = own, slots
+        self.send_sems, self.recv_sems, self.local_sem = send_sems, recv_sems, local_sem
+        self.sent = []
+
+    def index(self, z, y, c):
+        return (z * 2 + y) * 2 + c
+
+    def copy(self, source, origin, target):
+        sem = self.send_sems.at[len(self.sent)]
+        return pltpu.make_async_remote_copy(
+            src_ref=source,
+            dst_ref=self.slots.at[origin],
+            send_sem=sem,
+            recv_sem=self.recv_sems.at[origin],
+            device_id={"row": target},
+            device_id_type=MESH,
+        )
+
+    def send(self, source, origin, target, condition):
+        copy = self.copy(source, origin, target)
+        self.sent.append((condition, copy))
+        if condition is None:
+            copy.start()
+        else:
+            pl.when(condition)(copy.start)
+
+    def arrive(self, origin, condition):
+        z, y, c = self.place
+        copy = pltpu.make_async_remote_copy(
+            src_ref=self.slots.at[origin],
+            dst_ref=self.slots.at[origin],
+            send_sem=self.send_sems.at[0],
+            recv_sem=self.recv_sems.at[origin],
+            device_id={"row": self.index(z, y, 1 - c)},
+            device_id_type=MESH,
+        )
+        if condition is None:
+            copy.wait_recv()
+        else:
+            pl.when(condition)(copy.wait_recv)
+
+    def start(self):
+        z, y, c = self.place
+        me = self.index(z, y, c)
+        self.local = pltpu.make_async_copy(self.own, self.slots.at[me], self.local_sem)
+        self.local.start()
+        up, down = z + 1 < self.depth, z >= 1
+        self.send(self.own, me, self.index(jnp.minimum(z + 1, self.depth - 1), y, c), up)
+        self.send(self.own, me, self.index(jnp.maximum(z - 1, 0), y, c), down)
+        self.send(self.own, me, self.index(z, 1 - y, c), None)
+        self.send(self.own, me, self.index(z, y, 1 - c), None)
+
+    def along_z(self, step):
+        z, y, c = self.place
+        for sign in (-1, 1):
+            at = z + sign * (1 + step)
+            here = (at >= 0) & (at < self.depth)
+            origin = self.index(jnp.clip(at, 0, self.depth - 1), y, c)
+            self.arrive(origin, here)
+            on = z - sign
+            further = here & (on >= 0) & (on < self.depth)
+            source = self.slots.at[origin]
+            if step < self.depth - 2:
+                self.send(
+                    source, origin, self.index(jnp.clip(on, 0, self.depth - 1), y, c), further
+                )
+            self.send(source, origin, self.index(z, 1 - y, c), here)
+            self.send(source, origin, self.index(z, y, 1 - c), here)
+
+    def along_y(self, step):
+        z, y, c = self.place
+        for sign in (-1, 1) if step else (1,):
+            at = z + sign * step
+            here = (at >= 0) & (at < self.depth) if step else None
+            origin = self.index(jnp.clip(at, 0, self.depth - 1), 1 - y, c)
+            self.arrive(origin, here)
+            self.send(self.slots.at[origin], origin, self.index(z, y, 1 - c), here)
+
+    def finish(self):
+        z, y, c = self.place
+        for at in range(self.depth):
+            for side in range(2):
+                self.arrive(self.index(at, side, 1 - c), None)
+        self.local.wait()
+
+    def drain(self):
+        for condition, copy in self.sent:
+            if condition is None:
+                copy.wait_send()
+            else:
+                pl.when(condition)(copy.wait_send)
+
+
+def sends_of(depth):
+    return 4 + 6 * (depth - 1) + 2 * depth
+
+
+def forward_kernel(
+    n, rank, chunks, lag,
+    x_ref, factor_ref, target_ref, gate_up_ref, down_ref, out_factor_ref,
+    outputs_ref, fitness_ref, all_fitness_ref, full_factor_ref, noise_ref,
+    weights, down, raw, wide, x_all, x_mixed, acc, hidden, proj_in, proj_out, loss_in, loss_out,
+    pair_out, pair_keep, pair_in, y_out, y_keep, y_in, z_out, z_keep, z_in, sums,
+    weight_sems, down_sem, raw_sems, local_sems,
+    x_send, x_recv, f_send, f_recv, p_send, p_recv, l_send, l_recv,
+    c_send, c_recv, y_send, y_recv, z_send, z_recv,
+):
+    depth = n // 4
+    me = lax.axis_index("row")
+    c = lax.rem(me, 2)
+    y = lax.rem(me // 2, 2)
+    z = me // 4
+    own_rows, width = x_ref.shape
+    members = n * own_rows
+    local_width = factor_ref.shape[0]
+    blocks = weights.shape[0]
+
+    loads = []
+    for j in range(blocks):
+        cut = pl.ds(j * LANES, LANES)
+        raw_copy = pltpu.make_async_copy(out_factor_ref.at[:, :, cut], raw.at[j], raw_sems.at[j])
+        raw_copy.start()
+        loads.append(raw_copy)
+    weight_loads = []
+    for j in range(blocks):
+        cut = pl.ds(j * LANES, LANES)
+        copy = pltpu.make_async_copy(gate_up_ref.at[:, :, cut], weights.at[j], weight_sems.at[j])
+        copy.start()
+        weight_loads.append(copy)
+    down_load = pltpu.make_async_copy(down_ref, down, down_sem)
+    down_load.start()
+
+    barrier = pltpu.get_barrier_semaphore()
+    for k in range(1, n):
+        pl.semaphore_signal(
+            barrier, inc=1, device_id={"row": lax.rem(me + k, n)}, device_id_type=MESH
+        )
+    pl.semaphore_wait(barrier, n - 1)
+
+    x_gather = Gather(depth, (z, y, c), x_ref, x_all, x_send, x_recv, local_sems.at[0])
+    f_gather = Gather(
+        depth, (z, y, c), factor_ref, full_factor_ref, f_send, f_recv, local_sems.at[1]
+    )
+    x_gather.start()
+
+    def split(j):
+        loads[j].wait()
+        wide[...] = raw.at[j].reshape(members * rank * 2, LANES)[...].astype(jnp.float32)
+        for r in range(rank):
+            for k in range(2):
+                part = wide[pl.ds(r * 2 + k, members, 2 * rank), :]
+                noise_ref[j, r * members:(r + 1) * members, k * LANES:(k + 1) * LANES] = (
+                    part.astype(jnp.bfloat16)
+                )
+
+    for step in range(depth - 1):
+        x_gather.along_z(step)
+        x_gather.along_y(step)
+        split(step)
+    x_gather.along_y(depth - 1)
+    x_gather.finish()
+    f_gather.start()
+
+    def to_all(source, slots, send_sems, recv_sems):
+        copies = []
+        for k in range(1, n):
+            copy = pltpu.make_async_remote_copy(
+                src_ref=source,
+                dst_ref=slots.at[k],
+                send_sem=send_sems.at[k],
+                recv_sem=recv_sems.at[k],
+                device_id={"row": lax.rem(me + k, n)},
+                device_id_type=MESH,
+            )
+            copy.start()
+            copies.append(copy)
+        return copies
+
+    own_columns = pl.ds(pl.multiple_of(me * local_width, LANES), local_width)
+    x_own = x_all[:, :, own_columns].reshape(members, local_width)
+    crossed = jnp.dot(x_own, factor_ref[...], preferred_element_type=jnp.float32)
+    row_at = lax.broadcasted_iota(jnp.int32, (members, members), 0)
+    lane_at = lax.broadcasted_iota(jnp.int32, (members, members), 1)
+    proj_out[...] = jnp.zeros_like(proj_out)
+    for r in range(rank):
+        block = crossed[:, r * members:(r + 1) * members]
+        proj_out[r:r + 1, :] = jnp.sum(
+            jnp.where(row_at == lane_at, block, 0.0), axis=0, keepdims=True
+        )
+    proj_copies = to_all(proj_out, proj_in, p_send, p_recv)
+
+    spread_row = lax.broadcasted_iota(jnp.int32, (LANES, 2 * LANES), 0)
+    spread_lane = lax.broadcasted_iota(jnp.int32, (LANES, 2 * LANES), 1)
+    to_gate = jnp.where(spread_lane == 2 * spread_row, 1.0, 0.0).astype(jnp.bfloat16)
+    to_up = jnp.where(spread_lane == 2 * spread_row + 1, 1.0, 0.0).astype(jnp.bfloat16)
+
+    @pl.loop(0, width // LANES)
+    def _(i):
+        piece = x_all[:, :, pl.ds(pl.multiple_of(i * LANES, LANES), LANES)]
+        piece = piece.reshape(members, LANES)
+        cut = pl.ds(pl.multiple_of(i * 2 * LANES, LANES), 2 * LANES)
+        x_mixed[0:members, cut] = jnp.dot(
+            piece, to_gate, preferred_element_type=jnp.float32
+        ).astype(jnp.bfloat16)
+        x_mixed[members:2 * members, cut] = jnp.dot(
+            piece, to_up, preferred_element_type=jnp.float32
+        ).astype(jnp.bfloat16)
+
+    for j in range(depth - 1, blocks):
+        split(j)
+
+    for copy in proj_copies:
+        copy.wait()
+    projected = proj_out[...]
+    for k in range(1, n):
+        projected = projected + proj_in[k]
+    columns = [
+        jnp.sum(
+            jnp.where(row_at == lane_at, projected[r:r + 1, :], 0.0), axis=1, keepdims=True
+        )
+        for r in range(rank)
+    ]
+
+    deep = 2 * width // 8
+    for first in range(0, blocks, 2):
+        group = list(range(first, min(first + 2, blocks)))
+        for j in group:
+            weight_loads[j].wait()
+        views = [weights.at[j].reshape(2 * width, LANES) for j in group]
+        span = len(group) * LANES
+        acc[...] = jnp.zeros_like(acc)
+
+        @pl.loop(0, 2 * width // deep)
+        def _(i):
+            rows = pl.ds(pl.multiple_of(i * deep, LANES), deep)
+            w = [view[rows, :] for view in views]
+            w = jnp.concatenate(w, axis=1) if len(w) > 1 else w[0]
+            acc[:, 0:span] += jnp.dot(
+                x_mixed[:, rows], w, preferred_element_type=jnp.float32
+            )
+
+        for at, j in enumerate(group):
+            lanes = slice(at * LANES, (at + 1) * LANES)
+            two = []
+            for k in range(2):
+                noise = jnp.zeros((members, LANES), jnp.float32)
+                for r in range(rank):
+                    noise += columns[r] * noise_ref[
+                        j, r * members:(r + 1) * members, k * LANES:(k + 1) * LANES
+                    ].astype(jnp.float32)
+                two.append(
+                    acc[k * members:(k + 1) * members, lanes]
+                    + noise * (noise_scale / math.sqrt(rank))
+                )
+            hidden[:, j * LANES:(j + 1) * LANES] = (
+                (two[0] / (1.0 + jnp.exp(-two[0]))) * two[1]
+            ).astype(jnp.bfloat16)
+
+    f_gather.along_z(0)
+    f_gather.along_y(0)
+    down_load.wait()
+
+    span = width // chunks
+    sibling, across = (z * 2 + y) * 2 + 1 - c, (z * 2 + 1 - y) * 2 + c
+    pair_copies, y_copies, z_copies = [], [], []
+
+    def down_step(i):
+        part = jnp.dot(
+            hidden[...], down[:, i * span:(i + 1) * span], preferred_element_type=jnp.float32
+        ).reshape(2 * depth, 2, own_rows, span)
+        first, second = part[:, 0], part[:, 1]
+        pair_keep[i] = jnp.where(c == 0, first, second)
+        pair_out[i] = jnp.where(c == 0, second, first)
+        copy = pltpu.make_async_remote_copy(
+            src_ref=pair_out.at[i], dst_ref=pair_in.at[i],
+            send_sem=c_send.at[i], recv_sem=c_recv.at[i],
+            device_id={"row": sibling}, device_id_type=MESH,
+        )
+        copy.start()
+        pair_copies.append(copy)
+
+    def y_step(i):
+        pair_copies[i].wait_recv()
+        part = (pair_keep[i] + pair_in[i]).reshape(depth, 2, own_rows, span)
+        first, second = part[:, 0], part[:, 1]
+        y_keep[i] = jnp.where(y == 0, first, second)
+        y_out[i] = (
+            jnp.where(y == 0, second, first).reshape(depth * own_rows, span).astype(jnp.bfloat16)
+        )
+        copy = pltpu.make_async_remote_copy(
+            src_ref=y_out.at[i], dst_ref=y_in.at[i],
+            send_sem=y_send.at[i], recv_sem=y_recv.at[i],
+            device_id={"row": across}, device_id_type=MESH,
+        )
+        copy.start()
+        y_copies.append(copy)
+
+    def z_step(i):
+        y_copies[i].wait_recv()
+        part = y_keep[i] + y_in[i].astype(jnp.float32).reshape(depth, own_rows, span)
+        z_keep[i] = part
+        z_out[i] = part.astype(jnp.bfloat16)
+        copies = []
+        for k in range(1, depth):
+            to = lax.rem(z + k, depth)
+            copy = pltpu.make_async_remote_copy(
+                src_ref=z_out.at[i, to], dst_ref=z_in.at[i, k],
+                send_sem=z_send.at[i, k], recv_sem=z_recv.at[i, k],
+                device_id={"row": (to * 2 + y) * 2 + c}, device_id_type=MESH,
+            )
+            copy.start()
+            copies.append(copy)
+        z_copies.append(copies)
+
+    for t in range(chunks + 2 * lag):
+        if t < chunks:
+            down_step(t)
+        if 0 <= t - lag < chunks:
+            y_step(t - lag)
+        if 0 <= t - 2 * lag < chunks:
+            z_step(t - 2 * lag)
+        if t == chunks - 1:
+            for step in range(1, depth - 1):
+                f_gather.along_z(step)
+                f_gather.along_y(step)
+
+    total = jnp.zeros((own_rows, 1), jnp.float32)
+    for i in range(chunks):
+        part = z_keep[i, z]
+        for k in range(1, depth):
+            z_copies[i][k - 1].wait_recv()
+            part = part + z_in[i, k].astype(jnp.float32)
+        cut = slice(i * span, (i + 1) * span)
+        outputs_ref[:, cut] = part.astype(jnp.bfloat16)
+        miss = part - target_ref[:, cut]
+        total = total + jnp.sum(miss * miss, axis=1, keepdims=True)
+    loss_out[...] = jnp.broadcast_to(total / width, loss_out.shape)
+    loss_copies = to_all(loss_out, loss_in, l_send, l_recv)
+    f_gather.along_y(depth - 1)
+    for copy in loss_copies:
+        copy.wait()
+    loss_in[0] = loss_out[...]
+
+    def by_member(slot):
+        return loss_in[slot]
+
+    average = jnp.zeros((1, LANES), jnp.float32)
+    for k in range(n):
+        average = average + jnp.sum(loss_in[k], axis=0, keepdims=True)
+    average = average / members
+    spread = jnp.zeros((1, LANES), jnp.float32)
+    for k in range(n):
+        away = loss_in[k] - average
+        spread = spread + jnp.sum(away * away, axis=0, keepdims=True)
+    scale = jnp.sqrt(spread / members + 1e-06)
+    for d in range(n):
+        slot = lax.rem(me - d + n, n)
+        all_fitness_ref[d * own_rows:(d + 1) * own_rows, :] = (
+            average - loss_in[slot]
+        ) / scale
+    fitness_ref[...] = (average - loss_in[0]) / scale
+
+    f_gather.finish()
+    x_gather.drain()
+    f_gather.drain()
+    for copy in pair_copies + y_copies + [copy for some in z_copies for copy in some]:
+        copy.wait_send()
+
+
+def update_kernel(scale, rank, factor_ref, noise_ref, fitness_ref, update_ref, scaled):
+    members = fitness_ref.shape[0]
+    rows = update_ref.shape[0]
+
+    @pl.when(pl.program_id(1) == 0)
+    def _():
+        fitness = fitness_ref[...]
+        for r in range(rank):
+            for k in range(2):
+                at = (slice(r * members, (r + 1) * members), slice(k * LANES, (k + 1) * LANES))
+                scaled[at] = (
+                    fitness * noise_ref[(0,) + at].astype(jnp.float32)
+                ).astype(jnp.bfloat16)
+
+    start = pl.multiple_of(pl.program_id(1) * rows, LANES)
+    result = jnp.dot(
+        factor_ref[pl.ds(start, rows), :], scaled[...], preferred_element_type=jnp.float32
+    ) * scale
+    view = update_ref.reshape(2 * rows, LANES)
+    view[pl.ds(0, rows, 2), :] = result[:, :LANES]
+    view[pl.ds(1, rows, 2), :] = result[:, LANES:]
+
+
+def fast_body(n, members_in, gate_up, down_weight, factor_in, factor_out, target):
+    own_rows, width = members_in.shape
+    local_units = gate_up.shape[2]
+    members, rank, local_width = factor_in.shape
+    blocks = local_units // LANES
+    depth = n // 4
+    chunks, lag = 8, 2
+    span = width // chunks
+    factor = factor_in.transpose(2, 1, 0).reshape(local_width, rank * members)
+    rows_out = factor_out.reshape(members * rank, 2, local_units)
+    bf16, f32 = jnp.bfloat16, jnp.float32
+    dma = pltpu.SemaphoreType.DMA
+    vmem = pl.BlockSpec(memory_space=pltpu.VMEM)
+    hbm = pl.BlockSpec(memory_space=pl.ANY)
+    outputs, fitness, all_fitness, full_factor, noise = pl.pallas_call(
+        functools.partial(forward_kernel, n, rank, chunks, lag),
+        out_shape=(
+            jax.ShapeDtypeStruct((own_rows, width), bf16),
+            jax.ShapeDtypeStruct((own_rows, LANES), f32),
+            jax.ShapeDtypeStruct((members, LANES), f32),
+            jax.ShapeDtypeStruct((n, local_width, rank * members), bf16),
+            jax.ShapeDtypeStruct((blocks, rank * members, 2 * LANES), bf16),
+        ),
+        in_specs=[vmem, vmem, vmem, hbm, hbm, hbm],
+        out_specs=(vmem, vmem, vmem, hbm, vmem),
+        scratch_shapes=[
+            pltpu.VMEM((blocks, width, 2, LANES), bf16),
+            pltpu.VMEM((local_units, width), bf16),
+            pltpu.VMEM((blocks, members * rank, 2, LANES), bf16),
+            pltpu.VMEM((members * rank * 2, LANES), f32),
+            pltpu.VMEM((n, own_rows, width), bf16),
+            pltpu.VMEM((2 * members, 2 * width), bf16),
+            pltpu.VMEM((2 * members, 2 * LANES), f32),
+            pltpu.VMEM((members, local_units), bf16),
+            pltpu.VMEM((n, 8, members), f32),
+            pltpu.VMEM((8, members), f32),
+            pltpu.VMEM((n, own_rows, LANES), f32),
+            pltpu.VMEM((own_rows, LANES), f32),
+            pltpu.VMEM((chunks, 2 * depth, own_rows, span), f32),
+            pltpu.VMEM((chunks, 2 * depth, own_rows, span), f32),
+            pltpu.VMEM((chunks, 2 * depth, own_rows, span), f32),
+            pltpu.VMEM((chunks, depth * own_rows, span), bf16),
+            pltpu.VMEM((chunks, depth, own_rows, span), f32),
+            pltpu.VMEM((chunks, depth * own_rows, span), bf16),
+            pltpu.VMEM((chunks, depth, own_rows, span), bf16),
+            pltpu.VMEM((chunks, depth, own_rows, span), f32),
+            pltpu.VMEM((chunks, depth, own_rows, span), bf16),
+            pltpu.VMEM((8, LANES), f32),
+            dma((blocks,)), dma(()), dma((blocks,)), dma((2,)),
+            dma((sends_of(depth),)), dma((n,)),
+            dma((sends_of(depth),)), dma((n,)),
+            dma((n,)), dma((n,)), dma((n,)), dma((n,)),
+            dma((chunks,)), dma((chunks,)), dma((chunks,)), dma((chunks,)),
+            dma((chunks, depth)), dma((chunks, depth)),
+        ],
+        compiler_params=pltpu.CompilerParams(
+            collective_id=0, has_side_effects=True, vmem_limit_bytes=VMEM_LIMIT
+        ),
+        name="forward",
+    )(members_in, factor, target, gate_up, down_weight, rows_out)
+
+    block = width // 4
+    step_scale = math.sqrt(width / (members * rank))
+    update = pl.pallas_call(
+        functools.partial(update_kernel, step_scale, rank),
+        out_shape=jax.ShapeDtypeStruct((width, 2, local_units), f32),
+        grid=(blocks, width // block),
+        in_specs=[
+            pl.BlockSpec((width, rank * members), lambda j, i: (0, 0)),
+            pl.BlockSpec((1, rank * members, 2 * LANES), lambda j, i: (j, 0, 0)),
+            pl.BlockSpec((members, LANES), lambda j, i: (0, 0)),
+        ],
+        out_specs=pl.BlockSpec((block, 2, LANES), lambda j, i: (i, 0, j)),
+        scratch_shapes=[pltpu.VMEM((rank * members, 2 * LANES), bf16)],
+        compiler_params=pltpu.CompilerParams(vmem_limit_bytes=VMEM_LIMIT),
+        name="update",
+    )(full_factor.reshape(width, rank * members), noise, all_fitness)
+    return outputs, fitness[:, 0], update
+
+
+def body(n, members_in, gate_up, down_weight, factor_in, factor_out, target):
+    own_rows, width = members_in.shape
+    local_units = gate_up.shape[2]
+    members, rank, local_width = factor_in.shape
+    aligned = local_units % LANES == 0 and local_width % LANES == 0 and members == LANES
+    if aligned and n % 4 == 0 and n > 4 and own_rows == 8 and rank <= 8:
+        return fast_body(n, members_in, gate_up, down_weight, factor_in, factor_out, target)
+    return plain_body(members_in, gate_up, down_weight, factor_in, factor_out, target)
+
+
+def plain_body(members_in, gate_up, down_weight, factor_in, factor_out, target):
     own_rows = members_in.shape[0]
     width = gate_up.shape[0]
     local_units = gate_up.shape[2]
@@ -48,7 +539,7 @@
 
 def solution(mesh):
     return jax.shard_map(
-        body,
+        functools.partial(body, mesh.shape["row"]),
         mesh=mesh,
         in_specs=(
             P(("grp", "row"), None),

time: 295 us -> 116 us (0.39)
  waiting for transfers between devices: 119 us -> 0 us
  Pallas kernels: 0 us -> 111 us
  local copies, waits for them, and re-layouts: 81.2 us -> 3.89 us
  matrix products: 40.1 us -> 0 us
  blocking collectives: 29.7 us -> 0 us
  between operations: 15.8 us -> 0.65 us
  other arithmetic: 7.23 us -> 0 us
    pallas_call x0 -> x2, Pallas kernels: none -> 111 us  [the longest x1 87.2 us: fast_body(): pl.pallas_call(functools.partial(forward_kernel, n, rank, chunks, lag), o...]
    unnamed x13 -> x4, local copies, waits for them, and re-layouts: 60.9 us -> 1.37 us
    all_gather x2 -> x0, waiting for transfers between devices: 59.2 us -> none  [the longest x1 53.6 us: body(): full_factor = lax.all_gather(factor_in, 'row', axis=2, tiled=True)]
    reduce_scatter x1 -> x0, waiting for transfers between devices: 58.9 us -> none  [body(): lax.psum_scatter(jnp.dot(hidden, down_weight, preferred_element_type=jnp....]
    dot_general x4 -> x0, matrix products: 40.1 us -> none  [the longest x1 15.8 us: body(): lax.dot_general(full_factor, scaled, contract, preferred_element_type=jnp...]
    unnamed x1 -> x0, blocking collectives: 29.7 us -> none
    dot_general x1 -> x0, local copies, waits for them, and re-layouts: 19.6 us -> none  [body(): jnp.dot(whole_x, gate_up.reshape(width, 2 * local_units), preferred_eleme...]
    reduce_sum x4 -> x0, other arithmetic: 5.31 us -> none  [the longest x1 2.37 us: body(): noise = jnp.sum(projected[:, :, None, None] * factor_out, axis=1)]
  transfers between devices with their start and end apart: 3 -> 0, of which waited for: 3 -> 0; matrix products, arithmetic and copies ran while one was open for 13% -> 0% of each run, Pallas kernels for 0% -> 0%
where the time goes in v1:
time: 116 us
  Pallas kernels  111 us (96%)
  local copies, waits for them, and re-layouts  3.89 us (3%)
    pallas_call x1, Pallas kernels, fast_body(): pl.pallas_call(functools.partial(forward_kernel, n, rank, chunks, lag), o...  87.2 us
    pallas_call x1, Pallas kernels, fast_body(): pl.pallas_call(functools.partial(update_kernel, step_scale, rank), out_sh...  24.1 us

profile of v1, /device:TPU:0, one launch (start us, length us, event | category | flops | bytes accessed | tf_op | source)
XLA Modules:
  0.0 115.9 jit_solution(10699474647646919704)
XLA Ops:
  0.6 1.2 %copy.10 = bf16[256,4,128]{2,1,0:T(4,128)(2,1)S(1)} copy(bf16[256,4,128]{0,1,2:T(4,128)(2,1)} %bitcast.11) | data formatting | bytes 524288 | tf_op jit(solution)/shard_map/transpose | solution.py:420
  1.8 0.7 copy.13
  2.6 87.2 %forward.1 = (bf16[8,4096]{1,0:T(8,128)(2,1)}, f32[8,128]{1,0:T(8,128)}, f32[128,128]{1,0:T(8,128)}, bf16[16,256,512]{2,1,0:T(8,128)(2,1)}, bf16[7,512,256]{2,1,0:T(8,128)(2,1)}) custom-call(bf16[8,4096]{1,0:T(8,128)(2,1)} %x_ref.1, bf16[256,512]{1,0:T(8,128)(2,1)} %bitcast.9, f32[8,4096]{1,0:T(8,128)} %target_ref.1, bf16[4096,2,896]{2,1,0:T(2,128)(2,1)} %gate_up_ref.1, ...), custom_call_target="tpu_custom_call" | custom-call | tf_op jit(solution)/shard_map/forward/pallas_call | solution.py:426
  89.8 1.3 %slice_reduce_fusion = f32[8]{0:T(128)} fusion(f32[8,128]{1,0:T(8,128)} %get-tuple-element.9), kind=kLoop, calls=%fused_computation.1 | loop fusion | bytes 64 | tf_op jit(solution)/shard_map/slice | solution.py:489
  91.1 0.0 copy-start
  91.1 24.1 %update.1 = f32[4096,2,896]{2,1,0:T(2,128)} custom-call(bf16[4096,512]{1,0:T(8,128)(2,1)} %bitcast.7, bf16[7,512,256]{2,1,0:T(8,128)(2,1)} %get-tuple-element.11.noise_ref, f32[128,128]{1,0:T(8,128)} %get-tuple-element.12.fitness_ref), custom_call_target="tpu_custom_call" | custom-call | tf_op jit(solution)/shard_map/update/pallas_call | solution.py:475
  115.2 0.0 copy-done
  115.2 0.6 copy.15
Async XLA Ops:
  91.1 24.1 %copy-start = (bf16[8,4096]{1,0:T(8,128)(2,1)S(1)}, bf16[8,4096]{1,0:T(8,128)(2,1)}, u32[]{:S(2)}) copy-start(bf16[8,4096]{1,0:T(8,128)(2,1)} %get-tuple-element.16) | copy-start | bytes 196612

commit v2 on v1

--- a/solution.py
+++ b/solution.py
@@ -66,6 +66,10 @@
         up, down = z + 1 < self.depth, z >= 1
         self.send(self.own, me, self.index(jnp.minimum(z + 1, self.depth - 1), y, c), up)
         self.send(self.own, me, self.index(jnp.maximum(z - 1, 0), y, c), down)
+
+    def start_rest(self):
+        z, y, c = self.place
+        me = self.index(z, y, c)
         self.send(self.own, me, self.index(z, 1 - y, c), None)
         self.send(self.own, me, self.index(z, y, 1 - c), None)
 
@@ -161,6 +165,7 @@
         depth, (z, y, c), factor_ref, full_factor_ref, f_send, f_recv, local_sems.at[1]
     )
     x_gather.start()
+    x_gather.start_rest()
 
     def split(j):
         loads[j].wait()
@@ -176,9 +181,10 @@
         x_gather.along_z(step)
         x_gather.along_y(step)
         split(step)
+    f_gather.start()
     x_gather.along_y(depth - 1)
     x_gather.finish()
-    f_gather.start()
+    f_gather.start_rest()
 
     def to_all(source, slots, send_sems, recv_sems):
         copies = []
@@ -213,7 +219,7 @@
     to_gate = jnp.where(spread_lane == 2 * spread_row, 1.0, 0.0).astype(jnp.bfloat16)
     to_up = jnp.where(spread_lane == 2 * spread_row + 1, 1.0, 0.0).astype(jnp.bfloat16)
 
-    @pl.loop(0, width // LANES)
+    @pl.loop(0, width // LANES, unroll=4)
     def _(i):
         piece = x_all[:, :, pl.ds(pl.multiple_of(i * LANES, LANES), LANES)]
         piece = piece.reshape(members, LANES)
@@ -228,6 +234,30 @@
     for j in range(depth - 1, blocks):
         split(j)
 
+    deep = 2 * width // 4
+    for first in range(0, blocks, 2):
+        group = list(range(first, min(first + 2, blocks)))
+        for j in group:
+            weight_loads[j].wait()
+        views = [weights.at[j].reshape(2 * width, LANES) for j in group]
+        lanes = slice(first * LANES, (first + len(group)) * LANES)
+
+        def piece(i):
+            rows = pl.ds(pl.multiple_of(i * deep, LANES), deep)
+            w = [view[rows, :] for view in views]
+            w = jnp.concatenate(w, axis=1) if len(w) > 1 else w[0]
+            return jnp.dot(x_mixed[:, rows], w, preferred_element_type=jnp.float32)
+
+        acc[:, lanes] = piece(0)
+
+        @pl.loop(1, 2 * width // deep)
+        def _(i):
+            acc[:, lanes] += piece(i)
+
+        if first == 2:
+            f_gather.along_z(0)
+            f_gather.along_y(0)
+
     for copy in proj_copies:
         copy.wait()
     projected = proj_out[...]
@@ -240,43 +270,25 @@
         for r in range(rank)
     ]
 
-    deep = 2 * width // 8
-    for first in range(0, blocks, 2):
-        group = list(range(first, min(first + 2, blocks)))
-        for j in group:
-            weight_loads[j].wait()
-        views = [weights.at[j].reshape(2 * width, LANES) for j in group]
-        span = len(group) * LANES
-        acc[...] = jnp.zeros_like(acc)
-
-        @pl.loop(0, 2 * width // deep)
-        def _(i):
-            rows = pl.ds(pl.multiple_of(i * deep, LANES), deep)
-            w = [view[rows, :] for view in views]
-            w = jnp.concatenate(w, axis=1) if len(w) > 1 else w[0]
-            acc[:, 0:span] += jnp.dot(
-                x_mixed[:, rows], w, preferred_element_type=jnp.float32
+    for j in range(blocks):
+        lanes = slice(j * LANES, (j + 1) * LANES)
+        two = []
+        for k in range(2):
+            noise = jnp.zeros((members, LANES), jnp.float32)
+            for r in range(rank):
+                noise += columns[r] * noise_ref[
+                    j, r * members:(r + 1) * members, k * LANES:(k + 1) * LANES
+                ].astype(jnp.float32)
+            two.append(
+                acc[k * members:(k + 1) * members, lanes]
+                + noise * (noise_scale / math.sqrt(rank))
             )
-
-        for at, j in enumerate(group):
-            lanes = slice(at * LANES, (at + 1) * LANES)
-            two = []
-            for k in range(2):
-                noise = jnp.zeros((members, LANES), jnp.float32)
-                for r in range(rank):
-                    noise += columns[r] * noise_ref[
-                        j, r * members:(r + 1) * members, k * LANES:(k + 1) * LANES
-                    ].astype(jnp.float32)
-                two.append(
-                    acc[k * members:(k + 1) * members, lanes]
-                    + noise * (noise_scale / math.sqrt(rank))
-                )
-            hidden[:, j * LANES:(j + 1) * LANES] = (
-                (two[0] / (1.0 + jnp.exp(-two[0]))) * two[1]
-            ).astype(jnp.bfloat16)
-
-    f_gather.along_z(0)
-    f_gather.along_y(0)
+        hidden[:, j * LANES:(j + 1) * LANES] = (
+            (two[0] / (1.0 + jnp.exp(-two[0]))) * two[1]
+        ).astype(jnp.bfloat16)
+
+    f_gather.along_z(1)
+    f_gather.along_y(1)
     down_load.wait()
 
     span = width // chunks
@@ -338,8 +350,8 @@
             y_step(t - lag)
         if 0 <= t - 2 * lag < chunks:
             z_step(t - 2 * lag)
-        if t == chunks - 1:
-            for step in range(1, depth - 1):
+        if t == chunks + lag - 1:
+            for step in range(2, depth - 1):
                 f_gather.along_z(step)
                 f_gather.along_y(step)
 
@@ -441,7 +453,7 @@
             pltpu.VMEM((members * rank * 2, LANES), f32),
             pltpu.VMEM((n, own_rows, width), bf16),
             pltpu.VMEM((2 * members, 2 * width), bf16),
-            pltpu.VMEM((2 * members, 2 * LANES), f32),
+            pltpu.VMEM((2 * members, local_units), f32),
             pltpu.VMEM((members, local_units), bf16),
             pltpu.VMEM((n, 8, members), f32),
             pltpu.VMEM((8, members), f32),
@@ -470,7 +482,7 @@
         name="forward",
     )(members_in, factor, target, gate_up, down_weight, rows_out)
 
-    block = width // 4
+    block = width
     step_scale = math.sqrt(width / (members * rank))
     update = pl.pallas_call(
         functools.partial(update_kernel, step_scale, rank),

time: 116 us -> 84.7 us (0.73)
  Pallas kernels: 111 us -> 80 us
    pallas_call x1, Pallas kernels: 87.2 us -> 64.4 us  [fast_body(): pl.pallas_call(functools.partial(forward_kernel, n, rank, chunks, lag), o...]
    pallas_call x1, Pallas kernels: 24.1 us -> 15.6 us  [fast_body(): pl.pallas_call(functools.partial(update_kernel, step_scale, rank), out_sh...]
where the time goes in v2:
time: 84.7 us; the launch traced here: 84.5 us
  Pallas kernels  80 us (94%)
  local copies, waits for them, and re-layouts  3.89 us (5%)
    pallas_call x1, Pallas kernels, fast_body(): pl.pallas_call(functools.partial(forward_kernel, n, rank, chunks, lag), o...  64.4 us
    pallas_call x1, Pallas kernels, fast_body(): pl.pallas_call(functools.partial(update_kernel, step_scale, rank), out_sh...  15.6 us

profile of v2, /device:TPU:0, one launch (start us, length us, event | category | flops | bytes accessed | tf_op | source)
XLA Modules:
  0.0 84.5 jit_solution(17507128150178676523)
XLA Ops:
  0.6 1.2 %copy.10 = bf16[256,4,128]{2,1,0:T(4,128)(2,1)S(1)} copy(bf16[256,4,128]{0,1,2:T(4,128)(2,1)} %bitcast.11) | data formatting | bytes 524288 | tf_op jit(solution)/shard_map/transpose | solution.py:432
  1.8 0.7 copy.13
  2.6 64.4 %forward.1 = (bf16[8,4096]{1,0:T(8,128)(2,1)}, f32[8,128]{1,0:T(8,128)}, f32[128,128]{1,0:T(8,128)}, bf16[16,256,512]{2,1,0:T(8,128)(2,1)}, bf16[7,512,256]{2,1,0:T(8,128)(2,1)}) custom-call(bf16[8,4096]{1,0:T(8,128)(2,1)} %x_ref.1, bf16[256,512]{1,0:T(8,128)(2,1)} %bitcast.9, f32[8,4096]{1,0:T(8,128)} %target_ref.1, bf16[4096,2,896]{2,1,0:T(2,128)(2,1)} %gate_up_ref.1, ...), custom_call_target="tpu_custom_call" | custom-call | tf_op jit(solution)/shard_map/forward/pallas_call | solution.py:438
  67.0 1.3 %slice_reduce_fusion = f32[8]{0:T(128)} fusion(f32[8,128]{1,0:T(8,128)} %get-tuple-element.9), kind=kLoop, calls=%fused_computation.1 | loop fusion | bytes 64 | tf_op jit(solution)/shard_map/slice | solution.py:501
  68.3 0.0 copy-start
  68.3 15.6 %update.1 = f32[4096,2,896]{2,1,0:T(2,128)} custom-call(bf16[4096,512]{1,0:T(8,128)(2,1)} %bitcast.7, bf16[7,512,256]{2,1,0:T(8,128)(2,1)} %get-tuple-element.11.noise_ref, f32[128,128]{1,0:T(8,128)} %get-tuple-element.12.fitness_ref), custom_call_target="tpu_custom_call" | custom-call | tf_op jit(solution)/shard_map/update/pallas_call | solution.py:487
  83.9 0.0 copy-done
  83.9 0.6 copy.15
Async XLA Ops:
  68.3 15.6 %copy-start = (bf16[8,4096]{1,0:T(8,128)(2,1)S(1)}, bf16[8,4096]{1,0:T(8,128)(2,1)}, u32[]{:S(2)}) copy-start(bf16[8,4096]{1,0:T(8,128)(2,1)} %get-tuple-element.16) | copy-start | bytes 196612

commit v3 on v2

--- a/solution.py
+++ b/solution.py
@@ -15,7 +15,8 @@
 
 
 class Gather:
-    def __init__(self, depth, place, own, slots, send_sems, recv_sems, local_sem):
+    def __init__(self, depth, place, own, slots, send_sems, recv_sems, local_sem, direct):
+        self.direct = direct
         self.depth, self.place = depth, place
         self.own, self.slots = own, slots
         self.send_sems, self.recv_sems, self.local_sem = send_sems, recv_sems, local_sem
@@ -63,9 +64,11 @@
         me = self.index(z, y, c)
         self.local = pltpu.make_async_copy(self.own, self.slots.at[me], self.local_sem)
         self.local.start()
-        up, down = z + 1 < self.depth, z >= 1
-        self.send(self.own, me, self.index(jnp.minimum(z + 1, self.depth - 1), y, c), up)
-        self.send(self.own, me, self.index(jnp.maximum(z - 1, 0), y, c), down)
+        for hop in range(1, self.depth if self.direct else 2):
+            for to in (z + hop, z - hop):
+                there = (to >= 0) & (to < self.depth)
+                target = self.index(jnp.clip(to, 0, self.depth - 1), y, c)
+                self.send(self.own, me, target, there)
 
     def start_rest(self):
         z, y, c = self.place
@@ -83,7 +86,7 @@
             on = z - sign
             further = here & (on >= 0) & (on < self.depth)
             source = self.slots.at[origin]
-            if step < self.depth - 2:
+            if step < self.depth - 2 and not self.direct:
                 self.send(
                     source, origin, self.index(jnp.clip(on, 0, self.depth - 1), y, c), further
                 )
@@ -160,9 +163,11 @@
         )
     pl.semaphore_wait(barrier, n - 1)
 
-    x_gather = Gather(depth, (z, y, c), x_ref, x_all, x_send, x_recv, local_sems.at[0])
+    x_gather = Gather(
+        depth, (z, y, c), x_ref, x_all, x_send, x_recv, local_sems.at[0], True
+    )
     f_gather = Gather(
-        depth, (z, y, c), factor_ref, full_factor_ref, f_send, f_recv, local_sems.at[1]
+        depth, (z, y, c), factor_ref, full_factor_ref, f_send, f_recv, local_sems.at[1], False
     )
     x_gather.start()
     x_gather.start_rest()
@@ -178,9 +183,10 @@
                 )
 
     for step in range(depth - 1):
+        split(step)
+    for step in range(depth - 1):
         x_gather.along_z(step)
         x_gather.along_y(step)
-        split(step)
     f_gather.start()
     x_gather.along_y(depth - 1)
     x_gather.finish()

time: 84.7 us -> 84.4 us (level)
  no operation moved by 1% of the time
where the time goes in v3:
time: 84.4 us; the launch traced here: 84.2 us
  Pallas kernels  79.7 us (94%)
  local copies, waits for them, and re-layouts  3.89 us (5%)
    pallas_call x1, Pallas kernels, fast_body(): pl.pallas_call(functools.partial(forward_kernel, n, rank, chunks, lag), o...  64.1 us
    pallas_call x1, Pallas kernels, fast_body(): pl.pallas_call(functools.partial(update_kernel, step_scale, rank), out_sh...  15.6 us

profile of v3, /device:TPU:0, one launch (start us, length us, event | category | flops | bytes accessed | tf_op | source)
XLA Modules:
  0.0 84.2 jit_solution(4742431040272708832)
XLA Ops:
  0.6 1.2 %copy.10 = bf16[256,4,128]{2,1,0:T(4,128)(2,1)S(1)} copy(bf16[256,4,128]{0,1,2:T(4,128)(2,1)} %bitcast.11) | data formatting | bytes 524288 | tf_op jit(solution)/shard_map/transpose | solution.py:438
  1.8 0.7 copy.13
  2.6 64.1 %forward.1 = (bf16[8,4096]{1,0:T(8,128)(2,1)}, f32[8,128]{1,0:T(8,128)}, f32[128,128]{1,0:T(8,128)}, bf16[16,256,512]{2,1,0:T(8,128)(2,1)}, bf16[7,512,256]{2,1,0:T(8,128)(2,1)}) custom-call(bf16[8,4096]{1,0:T(8,128)(2,1)} %x_ref.1, bf16[256,512]{1,0:T(8,128)(2,1)} %bitcast.9, f32[8,4096]{1,0:T(8,128)} %target_ref.1, bf16[4096,2,896]{2,1,0:T(2,128)(2,1)} %gate_up_ref.1, ...), custom_call_target="tpu_custom_call" | custom-call | tf_op jit(solution)/shard_map/forward/pallas_call | solution.py:444
  66.7 1.3 %slice_reduce_fusion = f32[8]{0:T(128)} fusion(f32[8,128]{1,0:T(8,128)} %get-tuple-element.9), kind=kLoop, calls=%fused_computation.1 | loop fusion | bytes 64 | tf_op jit(solution)/shard_map/slice | solution.py:507
  68.0 0.0 copy-start
  68.0 15.6 %update.1 = f32[4096,2,896]{2,1,0:T(2,128)} custom-call(bf16[4096,512]{1,0:T(8,128)(2,1)} %bitcast.7, bf16[7,512,256]{2,1,0:T(8,128)(2,1)} %get-tuple-element.11.noise_ref, f32[128,128]{1,0:T(8,128)} %get-tuple-element.12.fitness_ref), custom_call_target="tpu_custom_call" | custom-call | tf_op jit(solution)/shard_map/update/pallas_call | solution.py:493
  83.6 0.0 copy-done
  83.6 0.6 copy.15
Async XLA Ops:
  68.0 15.6 %copy-start = (bf16[8,4096]{1,0:T(8,128)(2,1)S(1)}, bf16[8,4096]{1,0:T(8,128)(2,1)}, u32[]{:S(2)}) copy-start(bf16[8,4096]{1,0:T(8,128)(2,1)} %get-tuple-element.16) | copy-start | bytes 196612
